TPU v7x, 32 devices: a whole 2x2x4 slice. The times are simulated.
32 devices in a mesh: pt: 8 (over y, x, core), md: 4 (over z).
Axes of the slice: x: 2, y: 2, z: 4, core: 2. Of those that a mesh axis runs over, the one named last changes fastest.
Arguments:
- grid_index: int32 [3, 8192], P(None, 'pt'), may hold values from 0 to 255, as said below
- wavenumbers: int32 [3, 32768], P(None, 'md'), may hold values from -16 to 15, as said below
- test_block: int32 [32768, 256], P('md'), may hold values from -64 to 63
- slab_counts: int32 [8], P('pt'), may hold values from 1 to 1024, as said below
Outputs:
- adjoint_sketch: float32 [32768, 512], P(('md', 'pt'))
Inputs may be any that keep to these rules, and one draw needn't show every extreme that they name: Each slab's live points are its first slab_counts slots; in every draw one slab is full with 1024. `grid_index`: every slot's point lies in the ball of radius 256 // 2 - 1 about the grid cell (128, 128, 128). `wavenumbers`: the columns are the 32 x 32 x 32 tensor grid of wavenumber triples, each exactly once, in some order.
All inputs are finite; a program needn't handle non-finite values.
Results may differ from a plain program's by a relative error of at most 0.002.
Values may be sent and summed in bfloat16 or wider, within the bound.
A program may use at most 192 MiB of HBM per device.

v0:
```python
import math
import jax
import jax.numpy as jnp
from jax import lax
from jax.sharding import PartitionSpec as P

M = 32768
PERIOD = 512


def phase_pair(coords, wave_cols, row_start, block, live_rows):
    rows = lax.dynamic_slice_in_dim(coords, row_start, block, 1)
    turns = (
        rows[0][:, None] * wave_cols[0][None, :]
        + rows[1][:, None] * wave_cols[1][None, :]
        + rows[2][:, None] * wave_cols[2][None, :]
    )
    turns = jnp.mod(turns, PERIOD)
    angles = turns.astype(jnp.float32) * (2.0 * math.pi / PERIOD)
    in_use = row_start + jnp.arange(block, dtype=jnp.int32) < live_rows
    tile_re = jnp.where(in_use[:, None], jnp.cos(angles), 0.0).astype(jnp.bfloat16)
    tile_im = jnp.where(in_use[:, None], jnp.sin(angles), 0.0).astype(jnp.bfloat16)
    return (tile_re, tile_im)


def adjoint_piece(tile_re, tile_im, rows, width):
    dims = (((0,), (0,)), ((), ()))
    from_re = lax.dot_general(tile_re, rows, dims, preferred_element_type=jnp.float32)
    from_im = lax.dot_general(tile_im, rows, dims, preferred_element_type=jnp.float32)
    return jnp.concatenate(
        [from_re[:, :width] + from_im[:, width:], from_re[:, width:] - from_im[:, :width]], axis=1
    )


def per_device(grid_index, wavenumbers, test_block, slab_counts):
    capacity = grid_index.shape[1]
    width = test_block.shape[1]
    block = min(512, capacity)
    test_bf = test_block.astype(jnp.bfloat16)
    y_scale = 1.0 / (32.0 * math.sqrt(M))
    w_scale = 1.0 / math.sqrt(capacity * lax.axis_size("pt"))
    live_rows = slab_counts[0]
    block_count = (live_rows + block - 1) // block
    modes_local = wavenumbers.shape[1]

    def sketch_step(step_index, summed):
        row_start = step_index * block
        tile_re, tile_im = phase_pair(grid_index, wavenumbers, row_start, block, live_rows)
        part = jnp.concatenate(
            [
                jnp.dot(tile_re, test_bf, preferred_element_type=jnp.float32),
                jnp.dot(tile_im, test_bf, preferred_element_type=jnp.float32),
            ],
            axis=1,
        )
        return lax.dynamic_update_slice_in_dim(summed, part, row_start, 0)

    partial_value = lax.fori_loop(
        0, block_count, sketch_step, jnp.zeros((capacity, 2 * width), jnp.float32)
    )
    sketch = (lax.psum(partial_value, "md") * y_scale).astype(jnp.bfloat16)

    def fresh_step(step_index, summed):
        row_start = step_index * block
        tile_re, tile_im = phase_pair(grid_index, wavenumbers, row_start, block, live_rows)
        rows = lax.dynamic_slice_in_dim(sketch, row_start, block, 0)
        return summed + adjoint_piece(tile_re, tile_im, rows, width)

    summed = lax.fori_loop(
        0,
        block_count,
        fresh_step,
        jnp.zeros(
            (modes_local // lax.axis_size("pt") * lax.axis_size("pt"), 2 * width), jnp.float32
        ),
    )
    return lax.psum_scatter(summed * w_scale, "pt", scatter_dimension=0, tiled=True)


def solution(mesh):
    placed = (P(None, "pt"), P(None, "md"), P("md", None), P("pt"))
    return jax.shard_map(
        per_device, mesh=mesh, in_specs=placed, out_specs=P(("md", "pt"), None), check_vma=False
    )
```

profile of v0, /device:TPU:0, one launch (start us, length us, event | category | flops | bytes accessed | tf_op | source)
XLA Modules:
  0.0 944.1 jit_solution(14429266977389757838)
XLA Ops:
  6.5 0.0 all-reduce.2.cloned.1.call-start
  7.2 6.0 convert_element_type.42
  13.2 1.6 broadcast_in_dim.53.clone
  14.8 141.9 %while.24 = (s32[]{:T(128)}, f32[1024,512]{1,0:T(8,128)}, s32[]{:T(128)}, s32[]{:T(128)}, s32[3,1024]{1,0:T(4,128)}, /*index=5*/s32[3,8192]{1,0:T(4,128)}, bf16[...) while((s32[]{:T(128)}, f32[1024,512]{1,0:T(8,128)}, ...), condition=%wide.region_1.2_spmd, body=%wide.region_0.1_spmd.sunk | while | flops 4463002624 | bytes 66479860 | solution.py:58
  14.8 0.8 add_compare_fusion.4
  15.6 1.0 constant_dynamic-slice_fusion.4
  16.6 1.2 fusion.80
  17.8 65.0 %select_convert_fusion.25 = bf16[512,8192]{1,0:T(8,128)(2,1)S(1)} fusion(s32[8192]{0:T(1024)S(1)} %bitcast.60, s32[512]{0:T(512)S(1)} %bitcast.74, s32[8192]{0:T(1024)S(1)} %bitcast.62, s32[512]{0:T(512)S(1)} %bitcast.72, s32[8192]{0:T(1024)S(1)} %bitcast.58, s32[512]{0:T(512)S(1)} %bitcast.70, pred[512]{0:T(512)(128)(4,1)S(1)} %add_compare_fusion.4), kind=kLoop, calls=%fused_computation.7.clone.clone.1.clone.1 | loop fusion | flops 83886080 | bytes 8493568 | tf_op jit(solution)/shard_map/while/body/dot_general | solution.py:51
  82.8 4.6 fusion.82
  87.4 65.5 %select_convert_fusion.24 = bf16[512,8192]{1,0:T(8,128)(2,1)S(1)} fusion(s32[8192]{0:T(1024)S(1)} %bitcast.61, s32[512]{0:T(512)S(1)} %bitcast.75, s32[8192]{0:T(1024)S(1)} %bitcast.63, s32[512]{0:T(512)S(1)} %bitcast.73, s32[8192]{0:T(1024)S(1)} %bitcast.59, s32[512]{0:T(512)S(1)} %bitcast.71, pred[512]{0:T(512)(128)(4,1)S(1)} %add_compare_fusion.4), kind=kLoop, calls=%fused_computation.6.clone.clone.1.clone.1 | loop fusion | flops 83886080 | bytes 8493568 | tf_op jit(solution)/shard_map/while/body/dot_general | solution.py:52
  152.9 0.0 copy-done.1
  152.9 2.4 fusion.81
  155.2 0.1 pad_maximum_fusion.2
  155.3 0.3 copy.10
  155.7 1.0 constant_dynamic-update-slice_fusion.2
  156.7 0.0 all-reduce.2.cloned.1.call-update
  156.7 0.0 reduce-scatter.2.cloned.1.call-start
  156.8 230.3 %all-reduce.2.cloned.1.call-done = f32[1024,512]{1,0:T(8,128)} async-done(((f32[1024,512]{1,0:T(8,128)}), f32[1024,512]{1,0:T(8,128)}) %all-reduce.2.cloned.1.call-update) | async-done | bytes 2097168 | tf_op jit(solution)/shard_map/psum | solution.py:61
  387.1 1.9 multiply_convert_fusion
  388.9 7.8 broadcast_in_dim.52
  396.7 199.6 %while.25 = (s32[]{:T(128)}, f32[8192,512]{0,1:T(8,128)}, s32[]{:T(128)}, s32[]{:T(128)}, s32[3,1024]{1,0:T(4,128)}, /*index=5*/s32[3,8192]{1,0:T(4,128)S(1)}, b...) while((s32[]{:T(128)}, f32[8192,512]{0,1:T(8,128)}, ...), condition=%wide.region_4.5_spmd, body=%wide.region_3.4_spmd.sunk | while | flops 8770290688 | bytes 137783024 | solution.py:69
  408.6 0.7 add_compare_fusion.5
  409.3 0.9 constant_dynamic-slice_fusion.5
  410.2 0.1 fusion.85
  410.4 67.4 %fusion.89 = f32[8192,512]{0,1:T(8,128)} fusion(s32[8192]{0:T(1024)S(1)} %bitcast.66, s32[512]{0:T(512)S(1)} %bitcast.80, s32[8192]{0:T(1024)S(1)} %bitcast.68, s32[512]{0:T(512)S(1)} %bitcast.78, s32[8192]{0:T(1024)S(1)} %bitcast.64, s32[512]{0:T(512)S(1)} %bitcast.76, pred[512]{0:T(512)(128)(4,1)S(1)} %add_compare_fusion.5, ...), kind=kOutput, calls=%fused_computation.37.clone.3 | convolution fusion | flops 4378853376 | bytes 17406464 | tf_op jit(solution)/shard_map/while/body/dot_general | solution.py:28
  477.7 81.0 %fusion.87 = f32[8192,512]{0,1:T(8,128)} fusion(s32[8192]{0:T(1024)S(1)} %bitcast.67, s32[512]{0:T(512)S(1)} %bitcast.81, s32[8192]{0:T(1024)S(1)} %bitcast.69, s32[512]{0:T(512)S(1)} %bitcast.79, s32[8192]{0:T(1024)S(1)} %bitcast.65, s32[512]{0:T(512)S(1)} %bitcast.77, pred[512]{0:T(512)(128)(4,1)S(1)} %add_compare_fusion.5, ...), kind=kOutput, calls=%fused_computation.38.clone.3 | convolution fusion | flops 4378853376 | bytes 17406464 | tf_op jit(solution)/shard_map/while/body/dot_general | solution.py:29
  558.7 18.0 %slice_add_fusion.2 = (f32[8192,256]{0,1:T(8,128)}, f32[8192,256]{0,1:T(8,128)}) fusion(f32[8192,512]{0,1:T(8,128)} %fusion.87, f32[8192,512]{0,1:T(8,128)} %fusion.89), kind=kLoop, calls=%fused_computation.40.clone.1 | loop fusion | flops 4194304 | bytes 50331648 | tf_op jit(solution)/shard_map/while/body/add | solution.py:31
  576.8 17.2 %maximum_add_fusion.2 = f32[8192,512]{0,1:T(8,128)} fusion(f32[8192,512]{0,1:T(8,128)} %get-tuple-element.404, f32[8192,256]{0,1:T(8,128)} %get-tuple-element.349, f32[8192,256]{0,1:T(8,128)} %get-tuple-element.350), kind=kLoop, calls=%fused_computation.34.clone.1 | loop fusion | flops 8388608 | bytes 50331648 | tf_op jit(solution)/shard_map/while/body/add | solution.py:67
  596.3 17.4 %copy.6 = f32[8192,512]{1,0:T(8,128)} copy(f32[8192,512]{0,1:T(8,128)} %get-tuple-element.192) | data formatting | bytes 33554432 | tf_op jit(solution)/shard_map/while | solution.py:69
  613.8 11.7 %broadcast_multiply_fusion = f32[8192,512]{1,0:T(8,128)} fusion(f32[8192,512]{1,0:T(8,128)} %copy.6), kind=kLoop, calls=%fused_computation.59 | loop fusion | flops 4194304 | bytes 33554432 | tf_op jit(solution)/shard_map/mul | solution.py:77
  625.5 0.0 reduce-scatter.2.cloned.1.call-update
  625.5 311.4 %reduce-scatter.2.cloned.1.call-done = f32[1024,512]{1,0:T(8,128)} async-done(((f32[8192,512]{1,0:T(8,128)}), f32[1024,512]{1,0:T(8,128)}) %reduce-scatter.2.cloned.1.call-update) | async-done | bytes 2097168 | tf_op jit(solution)/shard_map/reduce_scatter | solution.py:77
  (5 shorter events, 0.1 us)
Async XLA Ops:
  6.5 380.5 %all-reduce.2.cloned.1.call-start = ((), (), s32[]{:S(2)}) async-start(), calls=%async_computation.1 | async-start | bytes 4194304 | tf_op jit(solution)/shard_map/psum | solution.py:61
  14.8 138.1 %copy-start.1 = (bf16[8192,256]{1,0:T(8,128)(2,1)S(1)}, bf16[8192,256]{1,0:T(8,128)(2,1)}, u32[]{:S(2)}) copy-start(bf16[8192,256]{1,0:T(8,128)(2,1)} %get-tuple-element.383) | copy-start | bytes 12582916 | tf_op jit(solution)/shard_map/while
  156.7 240.0 %copy-start = (s32[3,8192]{1,0:T(4,128)S(1)}, s32[3,8192]{1,0:T(4,128)}, u32[]{:S(2)}) copy-start(s32[3,8192]{1,0:T(4,128)} %get-tuple-element.435) | copy-start | bytes 294916
  156.7 780.2 %reduce-scatter.2.cloned.1.call-start = ((), (), s32[]{:S(2)}) async-start(), calls=%async_computation.2 | async-start | bytes 18874368 | tf_op jit(solution)/shard_map/reduce_scatter | solution.py:77
Sparse Core Ops, SparseCore 0:
  156.8 230.1 all-reduce.1
  625.7 311.2 reduce-scatter.1
where the time goes:
time: 945 us; the launch traced here: 944 us
  waiting for transfers between devices  542 us (57%)
  other arithmetic  187 us (20%)
  matrix products  155 us (16%)
  local copies, waits for them, and re-layouts  31.4 us (3%)
  loops' own time  14.4 us (2%)
  between operations  14.4 us (2%)
    reduce_scatter x1, waiting for transfers between devices, per_device(): lax.psum_scatter(summed * w_scale, 'pt', scatter_dimension=0, tiled=True)  311 us
    psum x1, waiting for transfers between devices, per_device(): sketch = (lax.psum(partial_value, 'md') * y_scale).astype(jnp.bfloat16)  230 us
    dot_general x1, matrix products, adjoint_piece(): lax.dot_general(tile_im, rows, dims, preferred_element_type=jnp.float32)  81 us
    dot_general x1, matrix products, adjoint_piece(): lax.dot_general(tile_re, rows, dims, preferred_element_type=jnp.float32)  67.4 us
    dot_general x1, other arithmetic, sketch_step(): jnp.dot(tile_im, test_bf, preferred_element_type=jnp.float32)  65.5 us
    dot_general x1, other arithmetic, sketch_step(): jnp.dot(tile_re, test_bf, preferred_element_type=jnp.float32)  65 us
  transfers between devices with their start and end apart: 2, of which 2 were waited for; matrix products, arithmetic and copies ran while one was open for 0% of the time, Pallas kernels for 0%

commit v1 on v0

--- a/solution.py
+++ b/solution.py
@@ -58,7 +58,7 @@
     partial_value = lax.fori_loop(
         0, block_count, sketch_step, jnp.zeros((capacity, 2 * width), jnp.float32)
     )
-    sketch = (lax.psum(partial_value, "md") * y_scale).astype(jnp.bfloat16)
+    sketch = (jnp.sum(lax.all_gather(partial_value, "md"), axis=0) * y_scale).astype(jnp.bfloat16)
 
     def fresh_step(step_index, summed):
         row_start = step_index * block

time: 945 us -> 1010 us (1.069); the launches traced: 944 us -> 992 us
  waiting for transfers between devices: 542 us -> 577 us
  matrix products: 155 us -> 141 us
  loops' own time: 14.4 us -> 25.7 us
    all_gather x0 -> x1, waiting for transfers between devices: none -> 292 us  [per_device(): lax.all_gather(partial_value, 'md')]
    psum x1 -> x0, waiting for transfers between devices: 230 us -> none  [per_device(): sketch = (lax.psum(partial_value, 'md') * y_scale).astype(jnp.bfloat16)]
    reduce_scatter x1, waiting for transfers between devices: 311 us -> 284 us  [per_device(): lax.psum_scatter(summed * w_scale, 'pt', scatter_dimension=0, tiled=True)]
    dot_general x1, matrix products: 81 us -> 67.2 us  [adjoint_piece(): lax.dot_general(tile_im, rows, dims, preferred_element_type=jnp.float32)]
    another operation x1, loops' own time: 14.3 us -> 25.2 us  [per_device(): lax.fori_loop(0, block_count, fresh_step, jnp.zeros((modes_local // lax.a...]
    all_gather x0 -> x1, local copies, waits for them, and re-layouts: none -> 10.8 us  [per_device(): lax.all_gather(partial_value, 'md')]
where the time goes in v1:
time: 1010 us; the launch traced here: 992 us
  waiting for transfers between devices  577 us (57%)
  other arithmetic  194 us (19%)
  matrix products  141 us (14%)
  local copies, waits for them, and re-layouts  40.8 us (4%)
  loops' own time  25.7 us (3%)
  between operations  14.3 us (1%)
    all_gather x1, waiting for transfers between devices, per_device(): lax.all_gather(partial_value, 'md')  292 us
    reduce_scatter x1, waiting for transfers between devices, per_device(): lax.psum_scatter(summed * w_scale, 'pt', scatter_dimension=0, tiled=True)  284 us
    dot_general x1, matrix products, adjoint_piece(): lax.dot_general(tile_im, rows, dims, preferred_element_type=jnp.float32)  67.2 us
    dot_general x1, matrix products, adjoint_piece(): lax.dot_general(tile_re, rows, dims, preferred_element_type=jnp.float32)  66.8 us
    dot_general x1, other arithmetic, sketch_step(): jnp.dot(tile_im, test_bf, preferred_element_type=jnp.float32)  65.5 us
    dot_general x1, other arithmetic, sketch_step(): jnp.dot(tile_re, test_bf, preferred_element_type=jnp.float32)  65 us
    another operation x1, loops' own time, per_device(): lax.fori_loop(0, block_count, fresh_step, jnp.zeros((modes_local // lax.a...  25.2 us
  transfers between devices with their start and end apart: 2, of which 2 were waited for; matrix products, arithmetic and copies ran while one was open for 0% of the time, Pallas kernels for 0%

profile of v1, /device:TPU:0, one launch (start us, length us, event | category | flops | bytes accessed | tf_op | source)
XLA Modules:
  0.0 992.1 jit_solution(1939257350669611383)
XLA Ops:
  7.2 6.0 convert_element_type.42
  13.2 0.2 broadcast_in_dim.53
  13.5 141.0 %while.24 = (s32[]{:T(128)}, f32[1024,512]{0,1:T(8,128)S(1)}, s32[]{:T(128)}, s32[]{:T(128)}, s32[3,1024]{1,0:T(4,128)}, /*index=5*/s32[3,8192]{1,0:T(4,128)}, b...) while((s32[]{:T(128)}, f32[1024,512]{0,1:T(8,128)S(1)}, ...), condition=%wide.region_1.2_spmd, body=%wide.region_0.1_spmd.sunk | while | flops 4463002624 | bytes 62285556 | solution.py:58
  13.5 0.8 add_compare_fusion.4
  14.3 1.0 constant_dynamic-slice_fusion.4
  15.3 1.2 fusion.80
  16.5 65.0 %select_convert_fusion.25 = bf16[512,8192]{1,0:T(8,128)(2,1)S(1)} fusion(s32[8192]{0:T(1024)S(1)} %bitcast.62, s32[512]{0:T(512)S(1)} %bitcast.76, s32[8192]{0:T(1024)S(1)} %bitcast.64, s32[512]{0:T(512)S(1)} %bitcast.74, s32[8192]{0:T(1024)S(1)} %bitcast.60, s32[512]{0:T(512)S(1)} %bitcast.72, pred[512]{0:T(512)(128)(4,1)S(1)} %add_compare_fusion.4), kind=kLoop, calls=%fused_computation.7.clone.clone.1.clone.1 | loop fusion | flops 83886080 | bytes 8493568 | tf_op jit(solution)/shard_map/while/body/dot_general | solution.py:51
  81.5 4.6 fusion.82
  86.1 65.5 %select_convert_fusion.24 = bf16[512,8192]{1,0:T(8,128)(2,1)S(1)} fusion(s32[8192]{0:T(1024)S(1)} %bitcast.63, s32[512]{0:T(512)S(1)} %bitcast.77, s32[8192]{0:T(1024)S(1)} %bitcast.65, s32[512]{0:T(512)S(1)} %bitcast.75, s32[8192]{0:T(1024)S(1)} %bitcast.61, s32[512]{0:T(512)S(1)} %bitcast.73, pred[512]{0:T(512)(128)(4,1)S(1)} %add_compare_fusion.4), kind=kLoop, calls=%fused_computation.6.clone.clone.1.clone.1 | loop fusion | flops 83886080 | bytes 8493568 | tf_op jit(solution)/shard_map/while/body/dot_general | solution.py:52
  151.6 2.4 fusion.81
  153.9 0.1 maximum_dynamic-update-slice_fusion.2
  154.4 0.0 copy-start
  154.4 1.3 copy-done
  155.8 0.0 all-gather.3.cloned.1.call-update
  155.8 0.0 reduce-scatter.2.cloned.1.call-start
  155.8 292.1 %all-gather.3.cloned.1.call-done = f32[4096,512]{0,1:T(8,128)} async-done(((f32[1024,512]{0,1:T(8,128)}), f32[4096,512]{0,1:T(8,128)}) %all-gather.3.cloned.1.call-update) | async-done | bytes 8388624 | tf_op jit(solution)/shard_map/all_gather | solution.py:61
  447.9 10.8 %reshape.16 = f32[4,1024,512]{1,0,2:T(4,128)} reshape(f32[4096,512]{0,1:T(8,128)} %all-gather.3.cloned.1.call-done) | data formatting | bytes 16777216 | tf_op jit(solution)/shard_map/all_gather | solution.py:61
  458.7 8.5 reduce_sum.9
  467.2 0.3 multiply_convert_fusion
  467.5 7.8 broadcast_in_dim.52
  475.2 196.2 %while.25 = (s32[]{:T(128)}, f32[8192,512]{0,1:T(8,128)}, s32[]{:T(128)}, s32[]{:T(128)}, s32[3,1024]{1,0:T(4,128)}, /*index=5*/s32[3,8192]{1,0:T(4,128)S(1)}, b...) while((s32[]{:T(128)}, f32[8192,512]{0,1:T(8,128)}, ...), condition=%wide.region_4.5_spmd, body=%wide.region_3.4_spmd.sunk | while | flops 8770290688 | bytes 137783024 | solution.py:69
  498.8 0.7 add_compare_fusion.5
  499.5 0.9 constant_dynamic-slice_fusion.5
  500.4 0.1 fusion.85
  500.6 66.8 %fusion.89 = f32[8192,512]{0,1:T(8,128)} fusion(s32[8192]{0:T(1024)S(1)} %bitcast.68, s32[512]{0:T(512)S(1)} %bitcast.82, s32[8192]{0:T(1024)S(1)} %bitcast.70, s32[512]{0:T(512)S(1)} %bitcast.80, s32[8192]{0:T(1024)S(1)} %bitcast.66, s32[512]{0:T(512)S(1)} %bitcast.78, pred[512]{0:T(512)(128)(4,1)S(1)} %add_compare_fusion.5, ...), kind=kOutput, calls=%fused_computation.36.clone.3 | convolution fusion | flops 4378853376 | bytes 17406464 | tf_op jit(solution)/shard_map/while/body/dot_general | solution.py:28
  567.4 67.2 %fusion.87 = f32[8192,512]{0,1:T(8,128)} fusion(s32[8192]{0:T(1024)S(1)} %bitcast.69, s32[512]{0:T(512)S(1)} %bitcast.83, s32[8192]{0:T(1024)S(1)} %bitcast.71, s32[512]{0:T(512)S(1)} %bitcast.81, s32[8192]{0:T(1024)S(1)} %bitcast.67, s32[512]{0:T(512)S(1)} %bitcast.79, pred[512]{0:T(512)(128)(4,1)S(1)} %add_compare_fusion.5, ...), kind=kOutput, calls=%fused_computation.37.clone.3 | convolution fusion | flops 4378853376 | bytes 17406464 | tf_op jit(solution)/shard_map/while/body/dot_general | solution.py:29
  634.6 18.0 %slice_add_fusion.2 = (f32[8192,256]{0,1:T(8,128)}, f32[8192,256]{0,1:T(8,128)}) fusion(f32[8192,512]{0,1:T(8,128)} %fusion.87, f32[8192,512]{0,1:T(8,128)} %fusion.89), kind=kLoop, calls=%fused_computation.39.clone.1 | loop fusion | flops 4194304 | bytes 50331648 | tf_op jit(solution)/shard_map/while/body/add | solution.py:31
  652.6 17.3 %maximum_add_fusion.2 = f32[8192,512]{0,1:T(8,128)} fusion(f32[8192,512]{0,1:T(8,128)} %get-tuple-element.411, f32[8192,256]{0,1:T(8,128)} %get-tuple-element.356, f32[8192,256]{0,1:T(8,128)} %get-tuple-element.357), kind=kLoop, calls=%fused_computation.33.clone.1 | loop fusion | flops 8388608 | bytes 50331648 | tf_op jit(solution)/shard_map/while/body/add | solution.py:67
  671.4 17.4 %copy.7 = f32[8192,512]{1,0:T(8,128)} copy(f32[8192,512]{0,1:T(8,128)} %get-tuple-element.192) | data formatting | bytes 33554432 | tf_op jit(solution)/shard_map/while | solution.py:69
  688.9 11.7 %broadcast_multiply_fusion = f32[8192,512]{1,0:T(8,128)} fusion(f32[8192,512]{1,0:T(8,128)} %copy.7), kind=kLoop, calls=%fused_computation.58 | loop fusion | flops 4194304 | bytes 33554432 | tf_op jit(solution)/shard_map/mul | solution.py:77
  700.6 0.0 reduce-scatter.2.cloned.1.call-update
  700.6 284.5 %reduce-scatter.2.cloned.1.call-done = f32[1024,512]{1,0:T(8,128)} async-done(((f32[8192,512]{1,0:T(8,128)}), f32[1024,512]{1,0:T(8,128)}) %reduce-scatter.2.cloned.1.call-update) | async-done | bytes 2097168 | tf_op jit(solution)/shard_map/reduce_scatter | solution.py:77
  (7 shorter events, 0.1 us)
Async XLA Ops:
  6.5 441.4 %all-gather.3.cloned.1.call-start = ((), (), s32[]{:S(2)}) async-start(), calls=%async_computation.2 | async-start | bytes 10485760 | tf_op jit(solution)/shard_map/all_gather | solution.py:61
  13.5 138.1 %copy-start.2 = (bf16[8192,256]{1,0:T(8,128)(2,1)S(1)}, bf16[8192,256]{1,0:T(8,128)(2,1)}, u32[]{:S(2)}) copy-start(bf16[8192,256]{1,0:T(8,128)(2,1)} %get-tuple-element.390) | copy-start | bytes 12582916 | tf_op jit(solution)/shard_map/while
  154.4 1.3 copy-start
  155.8 829.3 %reduce-scatter.2.cloned.1.call-start = ((), (), s32[]{:S(2)}) async-start(), calls=%async_computation.1 | async-start | bytes 18874368 | tf_op jit(solution)/shard_map/reduce_scatter | solution.py:77
  458.7 16.5 %copy-start.1 = (s32[3,8192]{1,0:T(4,128)S(1)}, s32[3,8192]{1,0:T(4,128)}, u32[]{:S(2)}) copy-start(s32[3,8192]{1,0:T(4,128)} %get-tuple-element.443) | copy-start | bytes 294916
Sparse Core Ops, SparseCore 0:
  155.9 291.9 all-gather.2
  700.8 284.2 reduce-scatter.1
